TPU v7x, 32 devices: a whole 2x2x4 slice. The times are simulated.
32 devices in a mesh: tm: 4 (over x, core), cell: 8 (over z, y).
Axes of the slice: x: 2, y: 2, z: 4, core: 2. Of those that a mesh axis runs over, the one named last changes fastest.
Arguments:
- coords: float32 [4, 64, 4096], P('tm', None, 'cell'), may hold values from -8 to 8
- potentials: float32 [4, 4096], P('tm', 'cell'), may hold values from -6 to 202
Outputs:
- beliefs: float32 [4, 4096], P('tm', 'cell')
All inputs are finite; a program needn't handle non-finite values.
Results may differ from a plain program's by a relative error of at most 0.00011.
Values sent between devices are 32-bit elements; how exact they have to be, the bound alone decides.
A program may use at most 64 MiB of HBM per device.

v0:
```python
import math

import jax
import jax.numpy as jnp
from jax import lax
from jax.sharding import PartitionSpec as P

TIMES = 4


EPS = 1.0


def from_behind(value, axis, steps):
    count = lax.axis_size(axis)
    initial, last = (max(0, -steps), min(count, count - steps))
    return lax.ppermute(value, axis, [(source, source + steps) for source in range(initial, last)])


def score_core(targets, carry, sources, belief):
    cross = lax.dot_general(
        sources,
        targets,
        (((0,), (0,)), ((), ())),
        precision=lax.Precision.HIGHEST,
        preferred_element_type=jnp.float32,
    )
    dist = (
        jnp.sum(sources * sources, axis=0)[:, None]
        + jnp.sum(targets * targets, axis=0)[None, :]
        - 2.0 * cross
    )
    score = belief[:, None] - dist / EPS
    top, total = carry
    newtop = jnp.maximum(top, jnp.max(score, axis=0))
    total = jnp.sum(jnp.exp(score - newtop[None, :]), axis=0)
    return (newtop, total)


def fold_scores(targets, carry, piece):
    points, weights = piece
    return score_core(targets, carry, points[0], weights[0, 0])


def start_carry(count):
    return (jnp.full((count,), -1e30, jnp.float32), jnp.zeros((count,), jnp.float32))


def body(coords, potentials):
    own = coords[0]
    local = own.shape[1]
    pot = potentials[0]
    offset = math.log(local * lax.axis_size("cell"))
    here = lax.axis_index("tm")
    belief = pot
    earlier = from_behind(coords, "tm", 1)
    for step in range(TIMES - 1):
        before = from_behind(belief, "tm", 1)
        top, total = fold_scores(
            own,
            start_carry(local),
            (
                lax.all_gather(earlier, "cell", axis=2, tiled=True),
                lax.all_gather(before[None, None, :], "cell", axis=2, tiled=True),
            ),
        )
        result = top + jnp.log(total) - offset
        belief = jnp.where(here == step + 1, result + pot, belief)
    return belief[None, :]


def solution(mesh):
    return jax.shard_map(
        body,
        mesh=mesh,
        in_specs=(P("tm", None, "cell"), P("tm", "cell")),
        out_specs=P("tm", "cell"),
        check_vma=False,
    )
```

profile of v0, /device:TPU:2, one launch (start us, length us, event | category | flops | bytes accessed | tf_op | source)
XLA Modules:
  0.0 153.7 jit_solution(13415377045305886690)
XLA Ops:
  6.5 1.9 %collective-permute-start.1 = (f32[1,64,512]{2,1,0:T(8,128)}, f32[1,64,512]{2,1,0:T(8,128)S(1)}, u32[]{:S(2)}, u32[]{:S(2)}) collective-permute-start(f32[1,64,512]{2,1,0:T(8,128)} %param.2), channel_id=1, source_target_pairs={{0,8},{8,16},{16,24},{1,9},{9,17},{17,25},{2,10},{10,18},{18,26},{... | collective-permute-start | bytes 393224 | tf_op jit(solution)/shard_map/ppermute | solution.py:17
  8.5 4.6 %collective-permute-done.1 = f32[1,64,512]{2,1,0:T(8,128)S(1)} collective-permute-done((f32[1,64,512]{2,1,0:T(8,128)}, f32[1,64,512]{2,1,0:T(8,128)S(1)}, u32[]{:S(2)}, u32[]{:S(2)}) %collective-permute-start.1) | collective-permute-done | bytes 131104 | tf_op jit(solution)/shard_map/ppermute | solution.py:17
  13.0 0.6 copy-done.2
  13.7 0.0 all-gather.8.cloned.1.call-update
  13.7 1.9 %collective-permute-start = (f32[512]{0:T(512)}, f32[512]{0:T(512)S(1)}, u32[]{:S(2)}, u32[]{:S(2)}) collective-permute-start(f32[512]{0:T(512)} %bitcast.32), channel_id=1, source_target_pairs={{0,8},{8,16},{16,24},{1,9},{9,17},{17,25},{2,10},{10,18},{18,26},{... | collective-permute-start | bytes 6152 | tf_op jit(solution)/shard_map/ppermute | solution.py:17
  15.6 0.9 fusion.3
  16.6 2.2 %collective-permute-done = f32[512]{0:T(512)S(1)} collective-permute-done((f32[512]{0:T(512)}, f32[512]{0:T(512)S(1)}, u32[]{:S(2)}, u32[]{:S(2)}) %collective-permute-start) | collective-permute-done | bytes 2080 | tf_op jit(solution)/shard_map/ppermute | solution.py:17
  18.8 26.5 %all-gather.3 = f32[8,1,512]{2,1,0:T(1,128)S(1)} all-gather(f32[1,1,512]{2,1,0:T(1,128)S(1)} %bitcast.38), channel_id=2, replica_groups=mesh['tm'=4,'cell'=8] {'cell'}, dimensions={0}, use_global_device_ids=true | all-gather | bytes 18432 | tf_op jit(solution)/shard_map/all_gather | solution.py:64
  45.3 10.0 %all-gather.8.cloned.1.call-done = f32[1,64,4096]{2,1,0:T(8,128)} async-done(((f32[1,64,512]{2,1,0:T(8,128)}), f32[1,64,4096]{2,1,0:T(8,128)}) %all-gather.8.cloned.1.call-update) | async-done | bytes 1048592 | tf_op jit(solution)/shard_map/all_gather | solution.py:63
  55.3 1.3 fusion.1
  56.7 9.3 %subtract_reduce_fusion.2 = (f32[512]{0:T(512)S(1)}, f32[4096,512]{1,0:T(8,128)S(1)}) fusion(f32[4096]{0:T(1024)S(1)} %bitcast.30, f32[1,64,512]{2,1,0:T(8,128)} %param.2, f32[1,64,4096]{2,1,0:T(8,128)} %all-gather.8.cloned.1.call-done, f32[512]{0:T(512)S(1)} %fusion.3, f32[4096]{0:T(1024)S(1)} %fusion.1), kind=kOutput, calls=%fused_computation.6 | convolution fusion | flops 1621097984 | bytes 9605120 | tf_op jit(solution)/shard_map/dot_general | solution.py:21
  66.0 3.2 %copy-done = f32[4096,512]{1,0:T(8,128)} copy-done((f32[4096,512]{1,0:T(8,128)}, f32[4096,512]{1,0:T(8,128)S(1)}, u32[]{:S(2)}) %copy-start) | copy-done | bytes 8388632
  69.2 1.5 exponential_reduce_fusion.2
  70.8 1.9 %collective-permute-start.2 = (f32[512]{0:T(512)S(1)}, f32[512]{0:T(512)S(1)}, u32[]{:S(2)}, u32[]{:S(2)}) collective-permute-start(f32[512]{0:T(512)S(1)} %get-tuple-element.7), channel_id=1, source_target_pairs={{0,8},{8,16},{16,24},{1,9},{9,17},{17,25},{2,10},{10,18},{18,26},{... | collective-permute-start | bytes 6152 | tf_op jit(solution)/shard_map/ppermute | solution.py:17
  72.7 3.0 %collective-permute-done.2 = f32[512]{0:T(512)S(1)} collective-permute-done((f32[512]{0:T(512)S(1)}, f32[512]{0:T(512)S(1)}, u32[]{:S(2)}, u32[]{:S(2)}) %collective-permute-start.2) | collective-permute-done | bytes 2080 | tf_op jit(solution)/shard_map/ppermute | solution.py:17
  75.7 26.1 %all-gather.4 = f32[8,1,512]{2,1,0:T(1,128)S(1)} all-gather(f32[1,1,512]{2,1,0:T(1,128)S(1)} %bitcast.40), channel_id=3, replica_groups=mesh['tm'=4,'cell'=8] {'cell'}, dimensions={0}, use_global_device_ids=true | all-gather | bytes 18432 | tf_op jit(solution)/shard_map/all_gather | solution.py:64
  101.8 3.8 %subtract_reduce_fusion.1 = f32[512]{0:T(512)S(1)} fusion(f32[4096,512]{1,0:T(8,128)} %copy-done, f32[4096]{0:T(1024)S(1)} %bitcast.28), kind=kLoop, calls=%fused_computation.5 | loop fusion | flops 4193792 | bytes 8407040 | tf_op jit(solution)/shard_map/reduce_max | solution.py:35
  105.6 1.5 %exponential_reduce_fusion.1 = f32[512]{0:T(512)S(1)} fusion(f32[4096,512]{1,0:T(8,128)S(1)} %copy-done.1, f32[4096]{0:T(1024)S(1)} %bitcast.29, f32[512]{0:T(512)S(1)} %broadcast_maximum_fusion.1), kind=kLoop, calls=%fused_computation.1 | loop fusion | flops 6290944 | bytes 8409088 | tf_op jit(solution)/shard_map/reduce_sum | solution.py:36
  107.2 1.9 %collective-permute-start.3 = (f32[512]{0:T(512)S(1)}, f32[512]{0:T(512)S(1)}, u32[]{:S(2)}, u32[]{:S(2)}) collective-permute-start(f32[512]{0:T(512)S(1)} %get-tuple-element.5), channel_id=1, source_target_pairs={{0,8},{8,16},{16,24},{1,9},{9,17},{17,25},{2,10},{10,18},{18,26},{... | collective-permute-start | bytes 6152 | tf_op jit(solution)/shard_map/ppermute | solution.py:17
  109.1 3.0 %collective-permute-done.3 = f32[512]{0:T(512)S(1)} collective-permute-done((f32[512]{0:T(512)S(1)}, f32[512]{0:T(512)S(1)}, u32[]{:S(2)}, u32[]{:S(2)}) %collective-permute-start.3) | collective-permute-done | bytes 2080 | tf_op jit(solution)/shard_map/ppermute | solution.py:17
  112.1 26.1 %all-gather.5 = f32[8,1,512]{2,1,0:T(1,128)S(1)} all-gather(f32[1,1,512]{2,1,0:T(1,128)S(1)} %bitcast.39), channel_id=4, replica_groups=mesh['tm'=4,'cell'=8] {'cell'}, dimensions={0}, use_global_device_ids=true | all-gather | bytes 18432 | tf_op jit(solution)/shard_map/all_gather | solution.py:64
  138.2 3.8 %subtract_reduce_fusion = f32[512]{0:T(512)S(1)} fusion(f32[4096,512]{1,0:T(8,128)} %copy-done, f32[4096]{0:T(1024)S(1)} %bitcast.26), kind=kLoop, calls=%fused_computation.4 | loop fusion | flops 4193792 | bytes 8407040 | tf_op jit(solution)/shard_map/reduce_max | solution.py:35
  142.0 4.2 %exponential_reduce_fusion = f32[512]{0:T(512)S(1)} fusion(f32[4096,512]{1,0:T(8,128)} %copy-done, f32[4096]{0:T(1024)S(1)} %bitcast.27, f32[512]{0:T(512)S(1)} %broadcast_maximum_fusion), kind=kLoop, calls=%fused_computation | loop fusion | flops 6290944 | bytes 8409088 | tf_op jit(solution)/shard_map/reduce_sum | solution.py:36
  146.3 0.6 broadcast_select_fusion.2
  (13 shorter events, 0.1 us)
Async XLA Ops:
  6.5 48.8 %all-gather.8.cloned.1.call-start = ((), (), s32[]{:S(2)}) async-start(), calls=%async_computation | async-start | bytes 1179648 | tf_op jit(solution)/shard_map/all_gather | solution.py:63
  6.5 6.5 %collective-permute-start.1 = (f32[1,64,512]{2,1,0:T(8,128)}, f32[1,64,512]{2,1,0:T(8,128)S(1)}, u32[]{:S(2)}, u32[]{:S(2)}) collective-permute-start(f32[1,64,512]{2,1,0:T(8,128)} %param.2), channel_id=1, source_target_pairs={{0,8},{8,16},{16,24},{1,9},{9,17},{17,25},{2,10},{10,18},{18,26},{... | collective-permute-start | bytes 393224 | tf_op jit(solution)/shard_map/ppermute | solution.py:17
  13.0 0.6 copy-start.2
  13.7 5.1 %collective-permute-start = (f32[512]{0:T(512)}, f32[512]{0:T(512)S(1)}, u32[]{:S(2)}, u32[]{:S(2)}) collective-permute-start(f32[512]{0:T(512)} %bitcast.32), channel_id=1, source_target_pairs={{0,8},{8,16},{16,24},{1,9},{9,17},{17,25},{2,10},{10,18},{18,26},{... | collective-permute-start | bytes 6152 | tf_op jit(solution)/shard_map/ppermute | solution.py:17
  66.0 3.2 %copy-start = (f32[4096,512]{1,0:T(8,128)}, f32[4096,512]{1,0:T(8,128)S(1)}, u32[]{:S(2)}) copy-start(f32[4096,512]{1,0:T(8,128)S(1)} %get-tuple-element.10) | copy-start | bytes 25165828
  66.0 4.7 %copy-start.3 = (f32[1,512]{1,0:T(1,128)S(1)}, f32[1,512]{1,0:T(1,128)}, u32[]{:S(2)}) copy-start(f32[1,512]{1,0:T(1,128)} %param.3) | copy-start | bytes 6148
  70.8 4.9 %collective-permute-start.2 = (f32[512]{0:T(512)S(1)}, f32[512]{0:T(512)S(1)}, u32[]{:S(2)}, u32[]{:S(2)}) collective-permute-start(f32[512]{0:T(512)S(1)} %get-tuple-element.7), channel_id=1, source_target_pairs={{0,8},{8,16},{16,24},{1,9},{9,17},{17,25},{2,10},{10,18},{18,26},{... | collective-permute-start | bytes 6152 | tf_op jit(solution)/shard_map/ppermute | solution.py:17
  72.7 32.9 %copy-start.1 = (f32[4096,512]{1,0:T(8,128)S(1)}, f32[4096,512]{1,0:T(8,128)}, u32[]{:S(2)}) copy-start(f32[4096,512]{1,0:T(8,128)} %copy-done) | copy-start | bytes 25165828
  107.2 4.9 %collective-permute-start.3 = (f32[512]{0:T(512)S(1)}, f32[512]{0:T(512)S(1)}, u32[]{:S(2)}, u32[]{:S(2)}) collective-permute-start(f32[512]{0:T(512)S(1)} %get-tuple-element.5), channel_id=1, source_target_pairs={{0,8},{8,16},{16,24},{1,9},{9,17},{17,25},{2,10},{10,18},{18,26},{... | collective-permute-start | bytes 6152 | tf_op jit(solution)/shard_map/ppermute | solution.py:17
Sparse Core Ops, SparseCore 0:
  13.8 41.4 all-gather.7
where the time goes:
time: 154 us
  blocking collectives  78.7 us (51%)
  waiting for transfers between devices  22.8 us (15%)
  other arithmetic  17.8 us (12%)
  between operations  13.6 us (9%)
  matrix products  9.3 us (6%)
  starting transfers between devices  7.68 us (5%)
  local copies, waits for them, and re-layouts  3.85 us (2%)
    all_gather x3, blocking collectives, body(): lax.all_gather(before[None, None, :], 'cell', axis=2, tiled=True)  78.7 us
    ppermute x4, waiting for transfers between devices, from_behind(): lax.ppermute(value, axis, [(source, source + steps) for source in range(i...  12.7 us
    all_gather x1, waiting for transfers between devices, body(): lax.all_gather(earlier, 'cell', axis=2, tiled=True)  10 us
    dot_general x1, matrix products, score_core(): lax.dot_general(sources, targets, (((0,), (0,)), ((), ())), precision=lax...  9.3 us
    ppermute x4, starting transfers between devices, from_behind(): lax.ppermute(value, axis, [(source, source + steps) for source in range(i...  7.67 us
    reduce_max x2, other arithmetic, score_core(): newtop = jnp.maximum(top, jnp.max(score, axis=0))  7.65 us
    reduce_sum x3, other arithmetic, score_core(): total = jnp.sum(jnp.exp(score - newtop[None, :]), axis=0)  7.31 us
    unnamed x8, local copies, waits for them, and re-layouts  3.85 us
  transfers between devices with their start and end apart: 5, of which 5 were waited for; matrix products, arithmetic and copies ran while one was open for 1% of the time, Pallas kernels for 0%

commit v1 on v0

v1 whole, which is shorter than its diff:
```python
import functools
import math

import jax
import jax.numpy as jnp
from jax import lax
from jax.experimental import pallas as pl
from jax.experimental.pallas import tpu as pltpu
from jax.sharding import PartitionSpec as P

EPS = 1.0
LOG2E = math.log2(math.e) / EPS
LN2 = math.log(2.0) * EPS
CHUNKS = 4
MESH = pl.DeviceIdType.MESH


def kernel(
    n,
    times,
    coords_hbm,
    pot_hbm,
    out_ref,
    own,
    pot,
    block,
    beliefs,
    sent,
    split_y,
    split_x,
    score,
    x_sq,
    top,
    total,
    load_sem,
    coord_send,
    relay_send,
    coord_recv,
    belief_send,
    belief_recv,
):
    dim, local = own.shape
    half = n // 2
    rows = dim // CHUNKS
    t = lax.axis_index("tm")
    cell = lax.axis_index("cell")
    me = jnp.where(cell % 2 == 0, cell // 2, n - 1 - cell // 2)

    def cell_of(pos):
        return jnp.where(pos < half, 2 * pos, 2 * (n - 1 - pos) + 1)

    def at(group, shift):
        return (group, cell_of(lax.rem(me + shift + n, n)))

    load_own = pltpu.make_async_copy(coords_hbm.at[0], own, load_sem.at[0])
    load_pot = pltpu.make_async_copy(pot_hbm, pot, load_sem.at[1])
    load_own.start()
    load_pot.start()

    barrier = pltpu.get_barrier_semaphore()

    @pl.when(t > 0)
    def _():
        for shift in (1, n - 1):
            pl.semaphore_signal(barrier, inc=1, device_id=at(t, shift), device_id_type=MESH)

        @pl.loop(0, n)
        def _(shift):
            pl.semaphore_signal(barrier, inc=1, device_id=at(t - 1, shift), device_id_type=MESH)

    pl.semaphore_wait(barrier, jnp.where(t < times - 1, n, 0) + jnp.where(t > 0, 2, 0))

    def first_copy(kind, chunk):
        shift = (1, n - 1, 0)[kind]
        return pltpu.make_async_remote_copy(
            src_ref=coords_hbm.at[0, pl.ds(chunk * rows, rows)],
            dst_ref=block.at[shift, pl.ds(chunk * rows, rows)],
            send_sem=coord_send.at[kind, chunk],
            recv_sem=coord_recv.at[shift, chunk],
            device_id=at(t + 1, shift),
            device_id_type=MESH,
        )

    def belief_copy(source, shift):
        return pltpu.make_async_remote_copy(
            src_ref=source,
            dst_ref=beliefs.at[shift],
            send_sem=belief_send.at[shift],
            recv_sem=belief_recv.at[shift],
            device_id=at(t + 1, shift),
            device_id_type=MESH,
        )

    def relay(source_slot, target_slot, chunk, shift):
        return pltpu.make_async_remote_copy(
            src_ref=block.at[source_slot, pl.ds(chunk * rows, rows)],
            dst_ref=block.at[target_slot, pl.ds(chunk * rows, rows)],
            send_sem=relay_send.at[target_slot, chunk],
            recv_sem=coord_recv.at[target_slot, chunk],
            device_id=at(t, shift),
            device_id_type=MESH,
        )

    @pl.when(t < times - 1)
    def _():
        for chunk in range(CHUNKS):
            first_copy(0, chunk).start()
            first_copy(1, chunk).start()
        for chunk in range(CHUNKS):
            first_copy(2, chunk).start()

    load_pot.wait()

    @pl.when(t == 0)
    def _():
        @pl.loop(0, n)
        def _(shift):
            belief_copy(pot, shift).start()

    def forward(dist):
        right_in, left_in = dist, n - dist
        last = dist + 1 == half
        for chunk in range(CHUNKS):
            relay(right_in, right_in, chunk, 1).wait_recv()
            if chunk < CHUNKS // 2:
                relay(right_in, dist + 1, chunk, 1).start()
            else:

                @pl.when(jnp.logical_not(last))
                def _():
                    relay(right_in, dist + 1, chunk, 1).start()

            relay(left_in, left_in, chunk, 1).wait_recv()
            if chunk >= CHUNKS // 2:
                relay(left_in, n - dist - 1, chunk, n - 1).start()
            else:

                @pl.when(jnp.logical_not(last))
                def _():
                    relay(left_in, n - dist - 1, chunk, n - 1).start()

    def arrive(slot):
        for chunk in range(CHUNKS):
            relay(slot, slot, chunk, 1).wait_recv()

    def make_scores(slot):
        x = block[slot]
        hi = x.astype(jnp.bfloat16)
        lo = (x - hi.astype(jnp.float32)).astype(jnp.bfloat16)
        split_x[pl.ds(0, dim)] = hi
        split_x[pl.ds(dim, dim)] = lo
        split_x[pl.ds(2 * dim, dim)] = hi
        split_x[pl.ds(3 * dim, dim)] = lo
        x_sq[slot] = jnp.sum(x * x, axis=0, keepdims=True)
        score[slot] = lax.dot_general(
            split_y[...],
            split_x[...],
            (((1,), (0,)), ((), ())),
            preferred_element_type=jnp.float32,
        )

    tile = 32

    def fold(slot):
        row = LOG2E * (beliefs[slot] - x_sq[slot])

        @pl.loop(0, local // tile, unroll=4)
        def _(step):
            here = pl.ds(pl.multiple_of(step * tile, tile), tile)
            parts = [
                score[slot, here, pl.ds(k, 128)] + row[:, k : k + 128]
                for k in range(0, local, 128)
            ]
            old = top[here]
            new = old
            for part in parts:
                new = jnp.maximum(new, part)
            acc = total[here] * jnp.exp2(old - new)
            for part in parts:
                acc = acc + jnp.exp2(part - new)
            top[here] = new
            total[here] = acc

    def slot_of(step):
        near = (step + 1) // 2
        return jnp.where(step % 2 == 1, near, lax.rem(n - near, n))

    @pl.when(t > 0)
    def _():
        load_own.wait()
        turned = (own[...] * (2.0 * LOG2E)).T
        hi = turned.astype(jnp.bfloat16)
        lo = (turned - hi.astype(jnp.float32)).astype(jnp.bfloat16)
        split_y[:, 0:dim] = hi
        split_y[:, dim : 2 * dim] = hi
        split_y[:, 2 * dim : 3 * dim] = lo
        split_y[:, 3 * dim : 4 * dim] = lo
        top[...] = jnp.full_like(top, -1e30)
        total[...] = jnp.zeros_like(total)

        def consume(slot):
            make_scores(slot)

            @pl.when(t == 1)
            def _():
                belief_copy(pot, slot).wait_recv()
                fold(slot)

        @pl.loop(1, half)
        def _(dist):
            forward(dist)

            @pl.when(dist == 1)
            def _():
                arrive(0)
                consume(0)

            @pl.when(dist > 1)
            def _():
                @pl.loop(2 * dist - 3, 2 * dist - 1)
                def _(step):
                    consume(slot_of(step))

        @pl.loop(n - 3, n)
        def _(step):
            @pl.when(step == n - 1)
            def _():
                arrive(half)

            consume(slot_of(step))

        @pl.when(t > 1)
        def _():
            @pl.loop(0, n)
            def _(step):
                slot = slot_of(step)
                belief_copy(pot, slot).wait_recv()
                fold(slot)

        tops = top[...].T
        peak = jnp.max(tops, axis=0, keepdims=True)
        mass = jnp.sum(total[...].T * jnp.exp2(tops - peak), axis=0, keepdims=True)
        y = own[...]
        y_sq = jnp.sum(y * y, axis=0, keepdims=True)
        sent[...] = (
            LN2 * (peak + jnp.log2(mass)) - y_sq / EPS - math.log(n * local) + pot[...]
        )

        @pl.when(t < times - 1)
        def _():
            @pl.loop(0, n)
            def _(shift):
                belief_copy(sent, shift).start()

        out_ref[...] = sent[...]

        @pl.loop(1, half)
        def _(dist):
            last = dist + 1 == half
            for chunk in range(CHUNKS):
                if chunk < CHUNKS // 2:
                    relay(dist, dist + 1, chunk, 1).wait_send()
                else:

                    @pl.when(jnp.logical_not(last))
                    def _():
                        relay(dist, dist + 1, chunk, 1).wait_send()

                if chunk >= CHUNKS // 2:
                    relay(n - dist, n - dist - 1, chunk, n - 1).wait_send()
                else:

                    @pl.when(jnp.logical_not(last))
                    def _():
                        relay(n - dist, n - dist - 1, chunk, n - 1).wait_send()

    @pl.when(t == 0)
    def _():
        load_own.wait()
        out_ref[...] = pot[...]

    @pl.when(t < times - 1)
    def _():
        for chunk in range(CHUNKS):
            for kind in range(3):
                first_copy(kind, chunk).wait_send()

        @pl.loop(0, n)
        def _(shift):
            belief_copy(sent, shift).wait_send()


def body(n, times, coords, potentials):
    _, dim, local = coords.shape
    f32, bf16 = jnp.float32, jnp.bfloat16
    dma = pltpu.SemaphoreType.DMA
    return pl.pallas_call(
        functools.partial(kernel, n, times),
        out_shape=jax.ShapeDtypeStruct((1, local), f32),
        in_specs=[pl.BlockSpec(memory_space=pl.ANY)] * 2,
        out_specs=pl.BlockSpec(memory_space=pltpu.VMEM),
        scratch_shapes=[
            pltpu.VMEM((dim, local), f32),
            pltpu.VMEM((1, local), f32),
            pltpu.VMEM((n, dim, local), f32),
            pltpu.VMEM((n, 1, local), f32),
            pltpu.VMEM((1, local), f32),
            pltpu.VMEM((local, 4 * dim), bf16),
            pltpu.VMEM((4 * dim, local), bf16),
            pltpu.VMEM((n, local, local), f32),
            pltpu.VMEM((n, 1, local), f32),
            pltpu.VMEM((local, 128), f32),
            pltpu.VMEM((local, 128), f32),
            dma((2,)),
            dma((3, CHUNKS)),
            dma((n, CHUNKS)),
            dma((n, CHUNKS)),
            dma((n,)),
            dma((n,)),
        ],
        compiler_params=pltpu.CompilerParams(
            collective_id=0, has_side_effects=True, vmem_limit_bytes=60 * 1024 * 1024
        ),
        name="sweep",
    )(coords, potentials)


def solution(mesh):
    return jax.shard_map(
        functools.partial(body, mesh.shape["cell"], mesh.shape["tm"]),
        mesh=mesh,
        in_specs=(P("tm", None, "cell"), P("tm", "cell")),
        out_specs=P("tm", "cell"),
        check_vma=False,
    )
```

time: 154 us -> 30.2 us (0.20)
  the two profiles are of different devices: /device:TPU:2 before, /device:TPU:3 now
where the time goes in v1:
time: 30.2 us; the launch traced here: 30 us
  Pallas kernels  28.7 us (95%)
  local copies, waits for them, and re-layouts  1.26 us (4%)
    pallas_call x1, Pallas kernels, body(): pl.pallas_call(functools.partial(kernel, n, times), out_shape=jax.ShapeDt...  28.7 us
    unnamed x1, local copies, waits for them, and re-layouts  1.26 us

profile of v1, /device:TPU:3, one launch (start us, length us, event | category | flops | bytes accessed | tf_op | source)
XLA Modules:
  0.0 30.0 jit_solution(17743126514924844323)
XLA Ops:
  0.0 28.7 %sweep.1 = f32[1,512]{1,0:T(1,128)} custom-call(f32[1,64,512]{2,1,0:T(8,128)} %coords_hbm.1, f32[1,512]{1,0:T(1,128)} %pot_hbm.1), custom_call_target="tpu_custom_call" | custom-call | tf_op jit(solution)/shard_map/sweep/pallas_call | solution.py:297
  28.7 1.3 %copy.4 = f32[1,512]{1,0:T(1,128)} copy(f32[1,512]{1,0:T(1,128)} %sweep.1) | data formatting | bytes 4096

commit v2 on v1

--- a/solution.py
+++ b/solution.py
@@ -37,7 +37,9 @@
     relay_send,
     coord_recv,
     belief_send,
+    belief_relay,
     belief_recv,
+    ready,
 ):
     dim, local = own.shape
     half = n // 2
@@ -52,23 +54,20 @@
     def at(group, shift):
         return (group, cell_of(lax.rem(me + shift + n, n)))
 
+    barrier = pltpu.get_barrier_semaphore()
+
+    @pl.when(t > 0)
+    def _():
+        for shift in (0, 1, n - 1):
+            pl.semaphore_signal(barrier, inc=1, device_id=at(t - 1, shift), device_id_type=MESH)
+        for shift in (1, n - 1):
+            pl.semaphore_signal(barrier, inc=1, device_id=at(t, shift), device_id_type=MESH)
+
     load_own = pltpu.make_async_copy(coords_hbm.at[0], own, load_sem.at[0])
     load_pot = pltpu.make_async_copy(pot_hbm, pot, load_sem.at[1])
     load_own.start()
     load_pot.start()
-
-    barrier = pltpu.get_barrier_semaphore()
-
-    @pl.when(t > 0)
-    def _():
-        for shift in (1, n - 1):
-            pl.semaphore_signal(barrier, inc=1, device_id=at(t, shift), device_id_type=MESH)
-
-        @pl.loop(0, n)
-        def _(shift):
-            pl.semaphore_signal(barrier, inc=1, device_id=at(t - 1, shift), device_id_type=MESH)
-
-    pl.semaphore_wait(barrier, jnp.where(t < times - 1, n, 0) + jnp.where(t > 0, 2, 0))
+    pl.semaphore_wait(barrier, jnp.where(t < times - 1, 3, 0) + jnp.where(t > 0, 2, 0))
 
     def first_copy(kind, chunk):
         shift = (1, n - 1, 0)[kind]
@@ -81,6 +80,27 @@
             device_id_type=MESH,
         )
 
+    def first_belief(kind):
+        shift = (1, n - 1, 0)[kind]
+        return pltpu.make_async_remote_copy(
+            src_ref=pot_hbm,
+            dst_ref=beliefs.at[shift],
+            send_sem=belief_send.at[shift],
+            recv_sem=belief_recv.at[shift],
+            device_id=at(t + 1, shift),
+            device_id_type=MESH,
+        )
+
+    def pass_belief(source_slot, target_slot, shift):
+        return pltpu.make_async_remote_copy(
+            src_ref=beliefs.at[source_slot],
+            dst_ref=beliefs.at[target_slot],
+            send_sem=belief_relay.at[target_slot],
+            recv_sem=belief_recv.at[target_slot],
+            device_id=at(t, shift),
+            device_id_type=MESH,
+        )
+
     def belief_copy(source, shift):
         return pltpu.make_async_remote_copy(
             src_ref=source,
@@ -106,18 +126,18 @@
         for chunk in range(CHUNKS):
             first_copy(0, chunk).start()
             first_copy(1, chunk).start()
+
+            if chunk == 0:
+
+                @pl.when(t == 0)
+                def _():
+                    for kind in range(3):
+                        first_belief(kind).start()
+
         for chunk in range(CHUNKS):
             first_copy(2, chunk).start()
 
-    load_pot.wait()
-
-    @pl.when(t == 0)
-    def _():
-        @pl.loop(0, n)
-        def _(shift):
-            belief_copy(pot, shift).start()
-
-    def forward(dist):
+    def forward(dist, pieces):
         right_in, left_in = dist, n - dist
         last = dist + 1 == half
         for chunk in range(CHUNKS):
@@ -138,6 +158,21 @@
                 @pl.when(jnp.logical_not(last))
                 def _():
                     relay(left_in, n - dist - 1, chunk, n - 1).start()
+
+            if chunk == 0:
+
+                @pl.when(t == 1)
+                def _():
+                    pass_belief(right_in, right_in, 1).wait_recv()
+                    pass_belief(right_in, dist + 1, 1).start()
+                    pass_belief(left_in, left_in, 1).wait_recv()
+
+                    @pl.when(jnp.logical_not(last))
+                    def _():
+                        pass_belief(left_in, n - dist - 1, n - 1).start()
+
+            if chunk < len(pieces):
+                pieces[chunk]()
 
     def arrive(slot):
         for chunk in range(CHUNKS):
@@ -198,48 +233,68 @@
         top[...] = jnp.full_like(top, -1e30)
         total[...] = jnp.zeros_like(total)
 
-        def consume(slot):
+        def scores_of(slot):
             make_scores(slot)
 
+            @pl.when(t > 1)
+            def _():
+                pl.semaphore_signal(
+                    ready, inc=1, device_id=at(t - 1, n - slot), device_id_type=MESH
+                )
+
+        def first_fold(slot):
             @pl.when(t == 1)
             def _():
-                belief_copy(pot, slot).wait_recv()
                 fold(slot)
 
-        @pl.loop(1, half)
+        def await_belief(slot):
+            @pl.when(t == 1)
+            def _():
+                pass_belief(slot, slot, 1).wait_recv()
+
+        forward(1, ())
+        arrive(0)
+        await_belief(0)
+        scores_of(0)
+        first_fold(0)
+
+        @pl.loop(2, half)
         def _(dist):
-            forward(dist)
-
-            @pl.when(dist == 1)
-            def _():
-                arrive(0)
-                consume(0)
-
-            @pl.when(dist > 1)
-            def _():
-                @pl.loop(2 * dist - 3, 2 * dist - 1)
-                def _(step):
-                    consume(slot_of(step))
+            right, left = dist - 1, n - dist + 1
+            forward(
+                dist,
+                (
+                    lambda: scores_of(right),
+                    lambda: first_fold(right),
+                    lambda: scores_of(left),
+                    lambda: first_fold(left),
+                ),
+            )
 
         @pl.loop(n - 3, n)
         def _(step):
+            slot = slot_of(step)
+
             @pl.when(step == n - 1)
             def _():
                 arrive(half)
-
-            consume(slot_of(step))
+                await_belief(half)
+
+            scores_of(slot)
+            first_fold(slot)
 
         @pl.when(t > 1)
         def _():
             @pl.loop(0, n)
             def _(step):
                 slot = slot_of(step)
-                belief_copy(pot, slot).wait_recv()
+                belief_copy(sent, slot).wait_recv()
                 fold(slot)
 
         tops = top[...].T
         peak = jnp.max(tops, axis=0, keepdims=True)
         mass = jnp.sum(total[...].T * jnp.exp2(tops - peak), axis=0, keepdims=True)
+        load_pot.wait()
         y = own[...]
         y_sq = jnp.sum(y * y, axis=0, keepdims=True)
         sent[...] = (
@@ -248,15 +303,26 @@
 
         @pl.when(t < times - 1)
         def _():
+            pl.semaphore_wait(ready, n)
+
             @pl.loop(0, n)
-            def _(shift):
-                belief_copy(sent, shift).start()
+            def _(step):
+                belief_copy(sent, slot_of(n - 1 - step)).start()
 
         out_ref[...] = sent[...]
 
         @pl.loop(1, half)
         def _(dist):
             last = dist + 1 == half
+
+            @pl.when(t == 1)
+            def _():
+                pass_belief(dist, dist + 1, 1).wait_send()
+
+                @pl.when(jnp.logical_not(last))
+                def _():
+                    pass_belief(n - dist, n - dist - 1, n - 1).wait_send()
+
             for chunk in range(CHUNKS):
                 if chunk < CHUNKS // 2:
                     relay(dist, dist + 1, chunk, 1).wait_send()
@@ -277,6 +343,9 @@
     @pl.when(t == 0)
     def _():
         load_own.wait()
+        load_pot.wait()
+        for kind in range(3):
+            first_belief(kind).wait_send()
         out_ref[...] = pot[...]
 
     @pl.when(t < times - 1)
@@ -285,9 +354,11 @@
             for kind in range(3):
                 first_copy(kind, chunk).wait_send()
 
-        @pl.loop(0, n)
-        def _(shift):
-            belief_copy(sent, shift).wait_send()
+        @pl.when(t > 0)
+        def _():
+            @pl.loop(0, n)
+            def _(shift):
+                belief_copy(sent, shift).wait_send()
 
 
 def body(n, times, coords, potentials):
@@ -317,6 +388,8 @@
             dma((n, CHUNKS)),
             dma((n,)),
             dma((n,)),
+            dma((n,)),
+            pltpu.SemaphoreType.REGULAR,
         ],
         compiler_params=pltpu.CompilerParams(
             collective_id=0, has_side_effects=True, vmem_limit_bytes=60 * 1024 * 1024

time: 30.2 us -> 34 us (1.13)
  Pallas kernels: 28.7 us -> 32.6 us
    pallas_call x1, Pallas kernels: 28.7 us -> 32.6 us  [body(): pl.pallas_call(functools.partial(kernel, n, times), out_shape=jax.ShapeDt...]
where the time goes in v2:
time: 34 us; the launch traced here: 33.9 us
  Pallas kernels  32.6 us (96%)
  local copies, waits for them, and re-layouts  1.26 us (4%)
    pallas_call x1, Pallas kernels, body(): pl.pallas_call(functools.partial(kernel, n, times), out_shape=jax.ShapeDt...  32.6 us
    unnamed x1, local copies, waits for them, and re-layouts  1.26 us

profile of v2, /device:TPU:3, one launch (start us, length us, event | category | flops | bytes accessed | tf_op | source)
XLA Modules:
  0.0 33.9 jit_solution(6204851851210042925)
XLA Ops:
  0.0 32.6 %sweep.1 = f32[1,512]{1,0:T(1,128)} custom-call(f32[1,64,512]{2,1,0:T(8,128)} %coords_hbm.1, f32[1,512]{1,0:T(1,128)} %pot_hbm.1), custom_call_target="tpu_custom_call" | custom-call | tf_op jit(solution)/shard_map/sweep/pallas_call | solution.py:368
  32.6 1.3 %copy.4 = f32[1,512]{1,0:T(1,128)} copy(f32[1,512]{1,0:T(1,128)} %sweep.1) | data formatting | bytes 4096

commit v3 on v2

--- a/solution.py
+++ b/solution.py
@@ -39,7 +39,6 @@
     belief_send,
     belief_relay,
     belief_recv,
-    ready,
 ):
     dim, local = own.shape
     half = n // 2
@@ -233,15 +232,6 @@
         top[...] = jnp.full_like(top, -1e30)
         total[...] = jnp.zeros_like(total)
 
-        def scores_of(slot):
-            make_scores(slot)
-
-            @pl.when(t > 1)
-            def _():
-                pl.semaphore_signal(
-                    ready, inc=1, device_id=at(t - 1, n - slot), device_id_type=MESH
-                )
-
         def first_fold(slot):
             @pl.when(t == 1)
             def _():
@@ -255,7 +245,7 @@
         forward(1, ())
         arrive(0)
         await_belief(0)
-        scores_of(0)
+        make_scores(0)
         first_fold(0)
 
         @pl.loop(2, half)
@@ -264,9 +254,9 @@
             forward(
                 dist,
                 (
-                    lambda: scores_of(right),
+                    lambda: make_scores(right),
                     lambda: first_fold(right),
-                    lambda: scores_of(left),
+                    lambda: make_scores(left),
                     lambda: first_fold(left),
                 ),
             )
@@ -280,7 +270,7 @@
                 arrive(half)
                 await_belief(half)
 
-            scores_of(slot)
+            make_scores(slot)
             first_fold(slot)
 
         @pl.when(t > 1)
@@ -303,8 +293,6 @@
 
         @pl.when(t < times - 1)
         def _():
-            pl.semaphore_wait(ready, n)
-
             @pl.loop(0, n)
             def _(step):
                 belief_copy(sent, slot_of(n - 1 - step)).start()
@@ -367,7 +355,7 @@
     dma = pltpu.SemaphoreType.DMA
     return pl.pallas_call(
         functools.partial(kernel, n, times),
-        out_shape=jax.ShapeDtypeStruct((1, local), f32),
+        out_shape=pltpu.VMEM((1, local), f32),
         in_specs=[pl.BlockSpec(memory_space=pl.ANY)] * 2,
         out_specs=pl.BlockSpec(memory_space=pltpu.VMEM),
         scratch_shapes=[
@@ -389,7 +377,6 @@
             dma((n,)),
             dma((n,)),
             dma((n,)),
-            pltpu.SemaphoreType.REGULAR,
         ],
         compiler_params=pltpu.CompilerParams(
             collective_id=0, has_side_effects=True, vmem_limit_bytes=60 * 1024 * 1024

time: 34 us -> 27.7 us (0.81)
  Pallas kernels: 32.6 us -> 27 us
  local copies, waits for them, and re-layouts: 1.26 us -> 0.58 us
    pallas_call x1, Pallas kernels: 32.6 us -> 27 us  [body(): pl.pallas_call(functools.partial(kernel, n, times), out_shape=pltpu.VMEM(...]
    unnamed x1, local copies, waits for them, and re-layouts: 1.26 us -> 0.58 us
where the time goes in v3:
time: 27.7 us; the launch traced here: 27.6 us
  Pallas kernels  27 us (97%)
  local copies, waits for them, and re-layouts  0.58 us (2%)
    pallas_call x1, Pallas kernels, body(): pl.pallas_call(functools.partial(kernel, n, times), out_shape=pltpu.VMEM(...  27 us
    unnamed x1, local copies, waits for them, and re-layouts  0.58 us

profile of v3, /device:TPU:3, one launch (start us, length us, event | category | flops | bytes accessed | tf_op | source)
XLA Modules:
  0.0 27.6 jit_solution(6017822060134440523)
XLA Ops:
  0.0 27.0 %sweep.1 = f32[1,512]{1,0:T(1,128)S(1)} custom-call(f32[1,64,512]{2,1,0:T(8,128)} %coords_hbm.1, f32[1,512]{1,0:T(1,128)} %pot_hbm.1), custom_call_target="tpu_custom_call" | custom-call | tf_op jit(solution)/shard_map/sweep/pallas_call | solution.py:356
  27.0 0.6 %copy.4 = f32[1,512]{1,0:T(1,128)} copy(f32[1,512]{1,0:T(1,128)S(1)} %sweep.1) | data formatting | bytes 4096

commit v4 on v3

--- a/solution.py
+++ b/solution.py
@@ -195,14 +195,16 @@
 
     tile = 32
 
-    def fold(slot):
-        row = LOG2E * (beliefs[slot] - x_sq[slot])
-
-        @pl.loop(0, local // tile, unroll=4)
+    def fold(*slots):
+        rows_of = [LOG2E * (beliefs[slot] - x_sq[slot]) for slot in slots]
+        size = tile // len(slots)
+
+        @pl.loop(0, local // size, unroll=4)
         def _(step):
-            here = pl.ds(pl.multiple_of(step * tile, tile), tile)
+            here = pl.ds(pl.multiple_of(step * size, size), size)
             parts = [
                 score[slot, here, pl.ds(k, 128)] + row[:, k : k + 128]
+                for slot, row in zip(slots, rows_of)
                 for k in range(0, local, 128)
             ]
             old = top[here]
@@ -275,11 +277,17 @@
 
         @pl.when(t > 1)
         def _():
-            @pl.loop(0, n)
-            def _(step):
-                slot = slot_of(step)
-                belief_copy(sent, slot).wait_recv()
-                fold(slot)
+            belief_copy(sent, 0).wait_recv()
+            fold(0)
+
+            @pl.loop(1, half)
+            def _(dist):
+                belief_copy(sent, dist).wait_recv()
+                belief_copy(sent, n - dist).wait_recv()
+                fold(dist, n - dist)
+
+            belief_copy(sent, half).wait_recv()
+            fold(half)
 
         tops = top[...].T
         peak = jnp.max(tops, axis=0, keepdims=True)

time: 27.7 us -> 27.6 us (level)
  no operation moved by 1% of the time
where the time goes in v4:
time: 27.6 us; the launch traced here: 27.4 us
  Pallas kernels  26.8 us (97%)
  local copies, waits for them, and re-layouts  0.58 us (2%)
    pallas_call x1, Pallas kernels, body(): pl.pallas_call(functools.partial(kernel, n, times), out_shape=pltpu.VMEM(...  26.8 us
    unnamed x1, local copies, waits for them, and re-layouts  0.58 us

profile of v4, /device:TPU:3, one launch (start us, length us, event | category | flops | bytes accessed | tf_op | source)
XLA Modules:
  0.0 27.4 jit_solution(4748441209271602548)
XLA Ops:
  0.0 26.8 %sweep.1 = f32[1,512]{1,0:T(1,128)S(1)} custom-call(f32[1,64,512]{2,1,0:T(8,128)} %coords_hbm.1, f32[1,512]{1,0:T(1,128)} %pot_hbm.1), custom_call_target="tpu_custom_call" | custom-call | tf_op jit(solution)/shard_map/sweep/pallas_call | solution.py:364
  26.9 0.6 %copy.4 = f32[1,512]{1,0:T(1,128)} copy(f32[1,512]{1,0:T(1,128)S(1)} %sweep.1) | data formatting | bytes 4096
